TPU v7x, 512 devices: a whole 4x8x8 slice. The times are simulated.
512 devices in a mesh: dp: 8 (over z), context: 16 (over y, core), tensor: 4 (over x).
Axes of the slice: x: 4, y: 8, z: 8, core: 2. Of those that a mesh axis runs over, the one named last changes fastest.
Arguments:
- layer_input: bfloat16 [8, 8192, 4096], P('dp', 'context', 'tensor'), may hold values from -6 to 6
- queries: bfloat16 [8, 16, 8192, 128], P('dp', 'tensor', 'context'), may hold values from -6 to 6
- key_states: bfloat16 [8, 4, 8192, 128], P('dp', 'tensor', 'context'), may hold values from -6 to 6
- value_states: bfloat16 [8, 4, 8192, 128], P('dp', 'tensor', 'context'), may hold values from -6 to 6
- out_grad: bfloat16 [8, 16, 8192, 128], P('dp', 'tensor', 'context'), may hold values from -0.0234375 to 0.0234375
- log_sums: bfloat16 [8, 16, 8192], P('dp', 'tensor', 'context'), may hold values from 2 to 5
- grad_dots: bfloat16 [8, 16, 8192], P('dp', 'tensor', 'context'), may hold values from -0.1875 to 0.1875
- doc_stretches: int32 [8, 10], P('dp'), may hold values from 1 to 8, as said below
- stretch_order: int32 [8, 256], P('dp'), may hold values from 0 to 255, as said below
- sign_vector: int32 [32, 128], P('context'), may hold values from -1 to 1, as said below
- exponents: int32 [8, 32], P('dp', 'context'), may hold values from 0 to 3
Outputs:
- rotated_grad: float32 [32, 128, 1024], P('context', 'dp', 'tensor')
Inputs may be any that keep to these rules, and one draw needn't show every extreme that they name: `doc_stretches`: each row gives the lengths in units of 128 tokens of 10 documents; they sum to 64. The second document is one of the longest, exactly 8 units, and begins 512 - 128 tokens after a multiple of 512 tokens. `stretch_order`: each row is a permutation of the 256 sequence blocks. Sequence blocks d * 16 to d * 16 + 15 belong to index d of context; the 16 stored blocks of one index of context hold at most 1 block belonging to any one index. `sign_vector`: every entry is 1 or -1.
All inputs are finite; a program needn't handle non-finite values.
Results may differ from a plain program's by a relative error of at most 0.0075.
Values may be sent and summed in bfloat16 or wider, within the bound.
No kernel may reach another device: no remote copies, remote signals or barrier semaphores. Data moves between devices by JAX's collectives and lax.ppermute only.
A program may use at most 64 MiB of HBM per device.

v0:
```python
import math
import jax
import jax.numpy as jnp
from jax import lax
from jax.sharding import PartitionSpec as P

HD = 128
GROUP = 4
BLK = 32
PAD = 128
HB = 128


def passed_along(block, axis, distance):
    devices = range(lax.axis_size(axis))
    route = [(i - distance, i) for i in devices if i - distance in devices]
    return lax.ppermute(block, axis, route)


def hadamard_table(table_size):
    index_row = jnp.arange(table_size, dtype=jnp.int32)
    common = jnp.bitwise_and(index_row[:, None], index_row[None, :])
    parity = jnp.zeros((table_size, table_size), jnp.int32)
    for bit_pos in range(table_size.bit_length() - 1):
        parity = parity + jnp.bitwise_and(jnp.right_shift(common, bit_pos), 1)
    signed = 1 - 2 * jnp.bitwise_and(parity, 1)
    return signed.astype(jnp.float32) * float(table_size) ** (-0.5)


def doc_of(position, ends_row):
    return jnp.sum(((position // PAD)[:, None] >= ends_row[None, :]).astype(jnp.int32), axis=1)


def live_pairs(query_pos, query_doc, key_pos, key_doc):
    return (query_doc[:, None] == key_doc[None, :]) & (key_pos[None, :] <= query_pos[:, None])


def block_grads(query_blk, grad_blk, lse_blk, dots_blk, key_blk, value_blk, live):
    scale = HD ** (-0.5)
    scores = (
        jnp.einsum("ghqd,gkd->ghqk", query_blk, key_blk, preferred_element_type=jnp.float32) * scale
    )
    probs = jnp.where(
        live[None, None], jnp.exp(scores - lse_blk.astype(jnp.float32)[..., None]), 0.0
    )
    value_part = jnp.einsum(
        "ghqk,ghqd->gkd", probs.astype(jnp.bfloat16), grad_blk, preferred_element_type=jnp.float32
    )
    dprobs = jnp.einsum("ghqd,gkd->ghqk", grad_blk, value_blk, preferred_element_type=jnp.float32)
    dscores = (probs * (dprobs - dots_blk.astype(jnp.float32)[..., None])).astype(jnp.bfloat16)
    key_part = (
        jnp.einsum("ghqk,ghqd->gkd", dscores, query_blk, preferred_element_type=jnp.float32) * scale
    )
    return (key_part, value_part)


def per_device(
    layer_input,
    queries,
    key_states,
    value_states,
    out_grad,
    log_sums,
    grad_dots,
    doc_stretches,
    stretch_order,
    sign_vector,
    exponents,
):
    local_tokens = queries.shape[2]
    local_kv = key_states.shape[1]
    local_cols = 2 * local_kv * HD
    order_row = stretch_order[0]
    ends_row = jnp.cumsum(doc_stretches[0])
    groups = lax.axis_size("context")
    slot_count = local_tokens // BLK
    capacity = max(1, slot_count // groups)
    device_id = lax.axis_index("context")
    order_grid = order_row.reshape(groups, slot_count)
    own_order = lax.dynamic_slice_in_dim(order_row, device_id * slot_count, slot_count, 0)
    own_target = own_order // slot_count
    slot_ids = jnp.arange(slot_count, dtype=jnp.int32)
    earlier = slot_ids[None, :] < slot_ids[:, None]
    send_rank = jnp.sum(
        jnp.where(earlier & (own_target[None, :] == own_target[:, None]), 1, 0), axis=1
    )
    send_row = own_target * capacity + send_rank
    buffer_ids = jnp.arange(groups * capacity, dtype=jnp.int32)
    send_table = (buffer_ids[:, None] == send_row[None, :]).astype(jnp.bfloat16)
    wanted = device_id * slot_count + slot_ids
    stretch_ids = jnp.arange(order_row.shape[0], dtype=jnp.int32)
    stored_at = jnp.sum(
        jnp.where(order_row[None, :] == wanted[:, None], stretch_ids[None, :], 0), axis=1
    )
    source = stored_at // slot_count
    source_slot = stored_at % slot_count
    source_orders = jnp.take(order_grid, source, axis=0)
    same_target = source_orders // slot_count == device_id
    recv_rank = jnp.sum(
        jnp.where(same_target & (slot_ids[None, :] < source_slot[:, None]), 1, 0), axis=1
    )
    recv_row = source * capacity + recv_rank
    recv_table = (recv_row[:, None] == buffer_ids[None, :]).astype(jnp.bfloat16)

    def pack(array):
        blocks = array[0].reshape(array.shape[1], slot_count, -1)
        return jnp.einsum(
            "rt,htx->rhx", send_table, blocks, preferred_element_type=jnp.float32
        ).astype(jnp.bfloat16)

    def unpack(packed):
        placed = jnp.einsum(
            "sr,rhx->hsx", recv_table, packed, preferred_element_type=jnp.float32
        ).astype(jnp.bfloat16)
        return placed.reshape(packed.shape[1], local_tokens, -1)

    moved = (
        lax.all_to_all(pack(queries), "context", split_axis=0, concat_axis=0, tiled=True),
        lax.all_to_all(pack(out_grad), "context", split_axis=0, concat_axis=0, tiled=True),
        lax.all_to_all(pack(key_states), "context", split_axis=0, concat_axis=0, tiled=True),
        lax.all_to_all(pack(value_states), "context", split_axis=0, concat_axis=0, tiled=True),
        lax.all_to_all(pack(log_sums), "context", split_axis=0, concat_axis=0, tiled=True),
        lax.all_to_all(pack(grad_dots), "context", split_axis=0, concat_axis=0, tiled=True),
    )
    query_sorted = unpack(moved[0])
    grad_sorted = unpack(moved[1])
    key_sorted = unpack(moved[2])
    value_sorted = unpack(moved[3])
    lse_sorted = unpack(moved[4])[:, :, 0]
    dots_sorted = unpack(moved[5])[:, :, 0]
    total_len = local_tokens * groups
    longest_tokens = max(total_len // PAD // 8, local_tokens // PAD) * PAD
    reach = (local_tokens - PAD + longest_tokens - 1) // local_tokens
    query_list = [query_sorted]
    grad_list = [grad_sorted]
    lse_list = [lse_sorted]
    dots_list = [dots_sorted]
    for ahead in range(1, reach + 1):
        later = passed_along(
            (query_sorted, grad_sorted, lse_sorted, dots_sorted), "context", -ahead
        )
        query_list.append(later[0])
        grad_list.append(later[1])
        lse_list.append(later[2])
        dots_list.append(later[3])
    all_query = jnp.concatenate(query_list, axis=1)
    all_grad = jnp.concatenate(grad_list, axis=1)
    all_lse = jnp.concatenate(lse_list, axis=1)
    all_dots = jnp.concatenate(dots_list, axis=1)
    total_rows = all_query.shape[1]
    query_pos_all = device_id * local_tokens + jnp.arange(total_rows, dtype=jnp.int32)
    query_doc_all = doc_of(query_pos_all, ends_row)
    key_pos_own = device_id * local_tokens + jnp.arange(local_tokens, dtype=jnp.int32)
    key_doc_own = doc_of(key_pos_own, ends_row)
    step_len = math.gcd(total_rows, 640)

    def ahead_block(index_val, running):
        offset = index_val * step_len
        query_blk = lax.dynamic_slice_in_dim(all_query, offset, step_len, 1).reshape(
            local_kv, GROUP, step_len, HD
        )
        grad_blk = lax.dynamic_slice_in_dim(all_grad, offset, step_len, 1).reshape(
            local_kv, GROUP, step_len, HD
        )
        lse_blk = lax.dynamic_slice_in_dim(all_lse, offset, step_len, 1).reshape(
            local_kv, GROUP, step_len
        )
        dots_blk = lax.dynamic_slice_in_dim(all_dots, offset, step_len, 1).reshape(
            local_kv, GROUP, step_len
        )
        query_pos = lax.dynamic_slice_in_dim(query_pos_all, offset, step_len, 0)
        query_doc = lax.dynamic_slice_in_dim(query_doc_all, offset, step_len, 0)
        live = live_pairs(query_pos, query_doc, key_pos_own, key_doc_own)
        key_part, value_part = block_grads(
            query_blk, grad_blk, lse_blk, dots_blk, key_sorted, value_sorted, live
        )
        return (running[0] + key_part, running[1] + value_part)

    empty = jnp.zeros((local_kv, local_tokens, HD), jnp.float32)
    key_total, value_total = lax.fori_loop(0, total_rows // step_len, ahead_block, (empty, empty))
    stacked = jnp.stack([key_total, value_total], axis=1)
    sorted_rows = (
        jnp.transpose(stacked, (2, 0, 1, 3))
        .reshape(slot_count, BLK * local_cols)
        .astype(jnp.bfloat16)
    )
    outgoing = jnp.einsum(
        "sr,sx->rx", recv_table, sorted_rows, preferred_element_type=jnp.float32
    ).astype(jnp.bfloat16)
    returned = lax.all_to_all(outgoing, "context", split_axis=0, concat_axis=0, tiled=True)
    stored_rows = jnp.einsum(
        "rt,rx->tx", send_table, returned, preferred_element_type=jnp.float32
    ).astype(jnp.bfloat16)
    kv_local = stored_rows.reshape(local_tokens, local_cols)[None]
    full_input = lax.all_gather(layer_input, "tensor", axis=2, tiled=True)
    row_input = lax.all_to_all(full_input, "context", split_axis=2, concat_axis=1, tiled=True)
    span = row_input[0]
    member_grad = jnp.einsum(
        "td,tc->dc",
        span,
        lax.all_gather(kv_local, "context", axis=1, tiled=True)[0],
        preferred_element_type=jnp.float32,
    )
    local_blocks = sign_vector.shape[0]
    had = hadamard_table(HB)
    shaped = (
        member_grad.reshape(local_blocks, HB, local_cols)
        * sign_vector.astype(jnp.float32)[:, :, None]
    )
    rotated = jnp.einsum("ij,bjc->bic", had, shaped, precision=lax.Precision.HIGHEST)
    factor = 1.0 / jnp.left_shift(jnp.int32(1), exponents[0]).astype(jnp.float32)
    quantized = (rotated * factor[:, None, None]).astype(jnp.bfloat16)
    spread = lax.all_to_all(quantized[None], "dp", split_axis=2, concat_axis=0, tiled=True)
    return jnp.sum(spread.astype(jnp.float32), axis=0)


def solution(mesh):
    return jax.shard_map(
        per_device,
        mesh=mesh,
        in_specs=(
            P("dp", "context", "tensor"),
            P("dp", "tensor", "context", None),
            P("dp", "tensor", "context", None),
            P("dp", "tensor", "context", None),
            P("dp", "tensor", "context", None),
            P("dp", "tensor", "context"),
            P("dp", "tensor", "context"),
            P("dp", None),
            P("dp", None),
            P("context", None),
            P("dp", "context"),
        ),
        out_specs=P("context", "dp", "tensor"),
        check_vma=False,
    )
```

profile of v0, /device:TPU:6, one launch (start us, length us, event | category | flops | bytes accessed | tf_op | source)
XLA Modules:
  0.0 429.9 jit_solution(6349806971333252527)
XLA Ops:
  12.0 7.2 %all-to-all-start.2 = ((bf16[16,4,32]{2,1,0:T(4,128)(2,1)}), bf16[16,4,32]{2,1,0:T(4,128)(2,1)S(1)}, u32[]{:S(2)}, u32[]{:S(2)}) async-start(bf16[16,4,32]{2,1,0:T(4,128)(2,1)} %copy.89), calls=%async_computation.2 | async-start | bytes 32768 | tf_op jit(solution)/shard_map/all_to_all | solution.py:122
  22.9 4.0 all-to-all-done.2
  26.9 3.5 all-to-all-start.5
  38.2 7.1 %all-to-all-start = ((bf16[16,4,4096]{2,1,0:T(4,128)(2,1)}), bf16[16,4,4096]{2,1,0:T(4,128)(2,1)S(1)}, u32[]{:S(2)}, u32[]{:S(2)}) async-start(bf16[16,4,4096]{2,1,0:T(4,128)(2,1)} %copy.86), calls=%async_computation | async-start | bytes 1048576 | tf_op jit(solution)/shard_map/all_to_all | solution.py:118
  45.8 15.6 %all-to-all-done = bf16[16,4,4096]{2,1,0:T(4,128)(2,1)S(1)} async-done(((bf16[16,4,4096]{2,1,0:T(4,128)(2,1)}), bf16[16,4,4096]{2,1,0:T(4,128)(2,1)S(1)}, u32[]{:S(2)}, u32[]{:S(2)}) %all-to-all-start) | async-done | bytes 524320 | tf_op jit(solution)/shard_map/all_to_all | solution.py:118
  61.3 4.2 all-to-all-start.3
  71.3 8.8 %collective-permute-done.3 = bf16[4,512]{1,0:T(4,128)(2,1)S(1)} collective-permute-done((bf16[4,512]{1,0:T(4,128)(2,1)S(1)}, bf16[4,512]{1,0:T(4,128)(2,1)S(1)}, u32[]{:S(2)}, u32[]{:S(2)}) %collective-permute-start.3) | collective-permute-done | bytes 4128 | tf_op jit(solution)/shard_map/ppermute | solution.py:17
  83.4 9.8 %all-to-all-start.1 = ((bf16[16,2,2048]{2,1,0:T(2,128)(2,1)}), bf16[16,2,2048]{2,1,0:T(2,128)(2,1)S(1)}, u32[]{:S(2)}, u32[]{:S(2)}) async-start(bf16[16,2,2048]{2,1,0:T(2,128)(2,1)} %reshape.396), calls=%async_computation.1 | async-start | bytes 262144 | tf_op jit(solution)/shard_map/all_to_all | solution.py:120
  95.2 16.5 %all-to-all-done.1 = bf16[16,2,2048]{2,1,0:T(2,128)(2,1)S(1)} async-done(((bf16[16,2,2048]{2,1,0:T(2,128)(2,1)}), bf16[16,2,2048]{2,1,0:T(2,128)(2,1)S(1)}, u32[]{:S(2)}, u32[]{:S(2)}) %all-to-all-start.1) | async-done | bytes 131104 | tf_op jit(solution)/shard_map/all_to_all | solution.py:120
  111.8 5.7 %all-to-all-start.4 = ((bf16[16,2,2048]{2,1,0:T(2,128)(2,1)}), bf16[16,2,2048]{2,1,0:T(2,128)(2,1)S(1)}, u32[]{:S(2)}, u32[]{:S(2)}) async-start(bf16[16,2,2048]{2,1,0:T(2,128)(2,1)} %reshape.398), calls=%async_computation.4 | async-start | bytes 262144 | tf_op jit(solution)/shard_map/all_to_all | solution.py:121
  119.3 6.9 %all-to-all-done.4 = bf16[16,2,2048]{2,1,0:T(2,128)(2,1)S(1)} async-done(((bf16[16,2,2048]{2,1,0:T(2,128)(2,1)}), bf16[16,2,2048]{2,1,0:T(2,128)(2,1)S(1)}, u32[]{:S(2)}, u32[]{:S(2)}) %all-to-all-start.4) | async-done | bytes 131104 | tf_op jit(solution)/shard_map/all_to_all | solution.py:121
  126.7 2.3 pad_maximum_fusion
  130.3 44.5 %while.16 = (s32[]{:T(128)}, f32[1,512,128]{2,1,0:T(8,128)S(1)}, f32[1,512,128]{2,1,0:T(8,128)S(1)}, s32[1536]{0:T(1024)S(1)}, s32[512]{0:T(512)S(1)}, /*index=5...) while((s32[]{:T(128)}, f32[1,512,128]{2,1,0:T(8,128)S(1)}, ...), condition=%wide.region_7.8_spmd.clone, body=%wide.region_6.7_spmd.clone.sunk | while | flops 270796288 | bytes 5133045 | solution.py:180
  132.0 1.7 fusion.161
  139.4 1.7 fusion.161
  143.1 1.7 fusion.161
  146.8 1.7 fusion.161
  150.5 1.7 fusion.161
  154.2 1.7 fusion.161
  157.9 1.7 fusion.161
  165.4 1.7 fusion.161
  176.7 17.0 %all_to_all.66 = bf16[16,2,4096]{2,1,0:T(2,128)(2,1)S(1)} all-to-all(bf16[16,2,4096]{2,1,0:T(2,128)(2,1)S(1)} %reshape.400), channel_id=1, replica_groups=mesh['dp'=8,'context'=16,'tensor'=4] {'context'}, dimensions={0} | all-to-all | bytes 524288 | tf_op jit(solution)/shard_map/all_to_all | solution.py:190
  194.0 18.9 %copy.98 = bf16[1,512,4096]{1,0,2:T(2,128)(2,1)} copy(bf16[1,512,4096]{2,1,0:T(8,128)(2,1)} %all-gather.5.cloned.1.call-done) | data formatting | bytes 8388608 | tf_op jit(solution)/shard_map/all_gather | solution.py:195
  212.9 28.5 %reduce.7 = bf16[4096,512]{1,0:T(8,128)(2,1)} reduce(bf16[4096,1,512]{2,1,0:T(2,128)(2,1)} %bitcast.157, bf16[]{:T(256)} %broadcast.474), dimensions={1}, to_apply=%bitcast.136.reduce_sub_computation | reduce | bytes 8388610
  241.4 11.4 %reshape.394 = bf16[16,2,65536]{2,1,0:T(2,128)(2,1)} reshape(bf16[4096,512]{1,0:T(8,128)(2,1)} %reduce.7) | data formatting | bytes 8388608
  252.8 4.7 %all-to-all-start.7 = ((bf16[16,2,65536]{2,1,0:T(2,128)(2,1)}), bf16[16,2,65536]{2,1,0:T(2,128)(2,1)}, u32[]{:S(2)}, u32[]{:S(2)}) async-start(bf16[16,2,65536]{2,1,0:T(2,128)(2,1)} %reshape.394), calls=%async_computation.7 | async-start | bytes 8388608 | tf_op jit(solution)/shard_map/all_to_all | solution.py:196
  258.9 112.6 %all-to-all-done.7 = bf16[16,2,65536]{2,1,0:T(2,128)(2,1)} async-done(((bf16[16,2,65536]{2,1,0:T(2,128)(2,1)}), bf16[16,2,65536]{2,1,0:T(2,128)(2,1)}, u32[]{:S(2)}, u32[]{:S(2)}) %all-to-all-start.7) | async-done | bytes 4194336 | tf_op jit(solution)/shard_map/all_to_all | solution.py:196
  371.4 12.3 %reshape.395 = bf16[4096,1,512]{2,1,0:T(2,128)(2,1)} reshape(bf16[16,2,65536]{2,1,0:T(2,128)(2,1)} %all-to-all-done.7) | data formatting | bytes 8388608
  383.8 6.5 %copy.108 = bf16[1,512,4096]{1,2,0:T(8,128)(2,1)} copy(bf16[1,512,4096]{1,0,2:T(2,128)(2,1)} %bitcast.158) | data formatting | bytes 8388608
  390.3 6.4 %copy.99 = bf16[1,16,512,256]{3,2,1,0:T(8,128)(2,1)} copy(bf16[1,16,512,256]{2,3,1,0:T(8,128)(2,1)} %bitcast.159) | data formatting | bytes 8388608 | tf_op jit(solution)/shard_map/all_to_all | solution.py:196
  396.7 5.2 %fusion.34 = f32[256,256]{0,1:T(8,128)S(1)} fusion(bf16[8192,256]{1,0:T(8,128)(2,1)} %bitcast.160, bf16[1,8192,256]{2,1,0:T(8,128)(2,1)} %all-gather.3.cloned.1.call-done), kind=kOutput, calls=%fused_computation.48 | convolution fusion | flops 1073741824 | bytes 8650752 | tf_op jit(solution)/shard_map/td,tc->dc/dot_general | solution.py:198
  402.6 19.2 %all_to_all.67 = bf16[1,2,128,256]{3,1,0,2:T(2,128)(2,1)S(1)} all-to-all(bf16[1,2,128,256]{3,1,0,2:T(2,128)(2,1)S(1)} %copy.101), channel_id=1, replica_groups=mesh['dp'=8,'context'=16,'tensor'=4] {'dp'}, dimensions={2} | all-to-all | bytes 262144 | tf_op jit(solution)/shard_map/all_to_all | solution.py:213
  (206 shorter events, 66.0 us)
Async XLA Ops:
  7.4 13.5 %copy-start.3 = (s32[1,256]{1,0:T(1,128)S(1)}, s32[1,256]{1,0:T(1,128)}, u32[]{:S(2)}) copy-start(s32[1,256]{1,0:T(1,128)} %param.21) | copy-start | bytes 3076
  7.4 13.7 %copy-start.1 = (bf16[1,1,512,128]{3,2,1,0:T(8,128)(2,1)S(1)}, bf16[1,1,512,128]{3,2,1,0:T(8,128)(2,1)}, u32[]{:S(2)}) copy-start(bf16[1,1,512,128]{3,2,1,0:T(8,128)(2,1)} %param.15) | copy-start | bytes 393220
  7.4 13.9 %copy-start = (bf16[1,4,512,128]{3,2,1,0:T(8,128)(2,1)S(1)}, bf16[1,4,512,128]{3,2,1,0:T(8,128)(2,1)}, u32[]{:S(2)}) copy-start(bf16[1,4,512,128]{3,2,1,0:T(8,128)(2,1)} %param.17) | copy-start | bytes 1572868
  7.4 14.4 %copy-start.2 = (bf16[1,1,512,128]{3,2,1,0:T(8,128)(2,1)S(1)}, bf16[1,1,512,128]{3,2,1,0:T(8,128)(2,1)}, u32[]{:S(2)}) copy-start(bf16[1,1,512,128]{3,2,1,0:T(8,128)(2,1)} %param.16) | copy-start | bytes 393220
  7.4 14.5 %copy-start.4 = (bf16[1,4,512]{2,1,0:T(4,128)(2,1)S(1)}, bf16[1,4,512]{2,1,0:T(4,128)(2,1)}, u32[]{:S(2)}) copy-start(bf16[1,4,512]{2,1,0:T(4,128)(2,1)} %param.19) | copy-start | bytes 12292
  7.4 23.0 %copy-start.6 = (s32[1,10]{1,0:T(1,128)S(1)}, s32[1,10]{1,0:T(1,128)}, u32[]{:S(2)}) copy-start(s32[1,10]{1,0:T(1,128)} %param.20) | copy-start | bytes 124
  7.4 186.6 %all-gather.5.cloned.1.call-start = ((), (), s32[]{:S(2)}) async-start(), calls=%async_computation.10 | async-start | bytes 5242880 | tf_op jit(solution)/shard_map/all_gather | solution.py:195
  12.0 14.8 %all-to-all-start.2 = ((bf16[16,4,32]{2,1,0:T(4,128)(2,1)}), bf16[16,4,32]{2,1,0:T(4,128)(2,1)S(1)}, u32[]{:S(2)}, u32[]{:S(2)}) async-start(bf16[16,4,32]{2,1,0:T(4,128)(2,1)} %copy.89), calls=%async_computation.2 | async-start | bytes 32768 | tf_op jit(solution)/shard_map/all_to_all | solution.py:122
  26.9 11.3 %all-to-all-start.5 = ((bf16[16,4,32]{2,1,0:T(4,128)(2,1)}), bf16[16,4,32]{2,1,0:T(4,128)(2,1)S(1)}, u32[]{:S(2)}, u32[]{:S(2)}) async-start(bf16[16,4,32]{2,1,0:T(4,128)(2,1)} %copy.94), calls=%async_computation.5 | async-start | bytes 32768 | tf_op jit(solution)/shard_map/all_to_all | solution.py:123
  38.2 23.2 %all-to-all-start = ((bf16[16,4,4096]{2,1,0:T(4,128)(2,1)}), bf16[16,4,4096]{2,1,0:T(4,128)(2,1)S(1)}, u32[]{:S(2)}, u32[]{:S(2)}) async-start(bf16[16,4,4096]{2,1,0:T(4,128)(2,1)} %copy.86), calls=%async_computation | async-start | bytes 1048576 | tf_op jit(solution)/shard_map/all_to_all | solution.py:118
  61.3 22.0 %all-to-all-start.3 = ((bf16[16,4,4096]{2,1,0:T(4,128)(2,1)}), bf16[16,4,4096]{2,1,0:T(4,128)(2,1)S(1)}, u32[]{:S(2)}, u32[]{:S(2)}) async-start(bf16[16,4,4096]{2,1,0:T(4,128)(2,1)} %copy.91), calls=%async_computation.3 | async-start | bytes 1048576 | tf_op jit(solution)/shard_map/all_to_all | solution.py:119
  65.8 14.2 %collective-permute-start.3 = (bf16[4,512]{1,0:T(4,128)(2,1)S(1)}, bf16[4,512]{1,0:T(4,128)(2,1)S(1)}, u32[]{:S(2)}, u32[]{:S(2)}) collective-permute-start(bf16[4,512]{1,0:T(4,128)(2,1)S(1)} %squeeze_reshape.6), channel_id=1, source_target_pairs={{8,0},{12,4},{16,8},{20,12},{24,16},{28,20},{32,24},{36,28},{40,32... | collective-permute-start | bytes 12296 | tf_op jit(solution)/shard_map/ppermute | solution.py:17
  67.1 13.0 %collective-permute-start.2 = (bf16[4,512]{1,0:T(4,128)(2,1)S(1)}, bf16[4,512]{1,0:T(4,128)(2,1)S(1)}, u32[]{:S(2)}, u32[]{:S(2)}) collective-permute-start(bf16[4,512]{1,0:T(4,128)(2,1)S(1)} %squeeze_reshape.6), channel_id=1, source_target_pairs={{4,0},{8,4},{12,8},{16,12},{20,16},{24,20},{28,24},{32,28},{36,32}... | collective-permute-start | bytes 12296 | tf_op jit(solution)/shard_map/ppermute | solution.py:17
  68.7 48.7 %collective-permute-start.7 = (bf16[4,512]{1,0:T(4,128)(2,1)S(1)}, bf16[4,512]{1,0:T(4,128)(2,1)S(1)}, u32[]{:S(2)}, u32[]{:S(2)}) collective-permute-start(bf16[4,512]{1,0:T(4,128)(2,1)S(1)} %squeeze_reshape.7), channel_id=1, source_target_pairs={{8,0},{12,4},{16,8},{20,12},{24,16},{28,20},{32,24},{36,28},{40,32... | collective-permute-start | bytes 12296 | tf_op jit(solution)/shard_map/ppermute | solution.py:17
  70.0 48.8 %collective-permute-start.6 = (bf16[4,512]{1,0:T(4,128)(2,1)S(1)}, bf16[4,512]{1,0:T(4,128)(2,1)S(1)}, u32[]{:S(2)}, u32[]{:S(2)}) collective-permute-start(bf16[4,512]{1,0:T(4,128)(2,1)S(1)} %squeeze_reshape.7), channel_id=1, source_target_pairs={{4,0},{8,4},{12,8},{16,12},{20,16},{24,20},{28,24},{32,28},{36,32}... | collective-permute-start | bytes 12296 | tf_op jit(solution)/shard_map/ppermute | solution.py:17
  80.8 45.9 %collective-permute-start.1 = (bf16[4,512,128]{2,1,0:T(8,128)(2,1)S(1)}, bf16[4,512,128]{2,1,0:T(8,128)(2,1)S(1)}, u32[]{:S(2)}, u32[]{:S(2)}) collective-permute-start(bf16[4,512,128]{2,1,0:T(8,128)(2,1)S(1)} %reshape.358), channel_id=1, source_target_pairs={{8,0},{12,4},{16,8},{20,12},{24,16},{28,20},{32,24},{36,28},{40,32... | collective-permute-start | bytes 1572872 | tf_op jit(solution)/shard_map/ppermute | solution.py:17
  82.1 44.6 %collective-permute-start = (bf16[4,512,128]{2,1,0:T(8,128)(2,1)S(1)}, bf16[4,512,128]{2,1,0:T(8,128)(2,1)}, u32[]{:S(2)}, u32[]{:S(2)}) collective-permute-start(bf16[4,512,128]{2,1,0:T(8,128)(2,1)S(1)} %reshape.358), channel_id=1, source_target_pairs={{4,0},{8,4},{12,8},{16,12},{20,16},{24,20},{28,24},{32,28},{36,32}... | collective-permute-start | bytes 1572872 | tf_op jit(solution)/shard_map/ppermute | solution.py:17
  83.4 28.4 %all-to-all-start.1 = ((bf16[16,2,2048]{2,1,0:T(2,128)(2,1)}), bf16[16,2,2048]{2,1,0:T(2,128)(2,1)S(1)}, u32[]{:S(2)}, u32[]{:S(2)}) async-start(bf16[16,2,2048]{2,1,0:T(2,128)(2,1)} %reshape.396), calls=%async_computation.1 | async-start | bytes 262144 | tf_op jit(solution)/shard_map/all_to_all | solution.py:120
  93.9 35.1 %collective-permute-start.5 = (bf16[4,512,128]{2,1,0:T(8,128)(2,1)S(1)}, bf16[4,512,128]{2,1,0:T(8,128)(2,1)}, u32[]{:S(2)}, u32[]{:S(2)}) collective-permute-start(bf16[4,512,128]{2,1,0:T(8,128)(2,1)S(1)} %reshape.362), channel_id=1, source_target_pairs={{8,0},{12,4},{16,8},{20,12},{24,16},{28,20},{32,24},{36,28},{40,32... | collective-permute-start | bytes 1572872 | tf_op jit(solution)/shard_map/ppermute | solution.py:17
  111.8 14.4 %all-to-all-start.4 = ((bf16[16,2,2048]{2,1,0:T(2,128)(2,1)}), bf16[16,2,2048]{2,1,0:T(2,128)(2,1)S(1)}, u32[]{:S(2)}, u32[]{:S(2)}) async-start(bf16[16,2,2048]{2,1,0:T(2,128)(2,1)} %reshape.398), calls=%async_computation.4 | async-start | bytes 262144 | tf_op jit(solution)/shard_map/all_to_all | solution.py:121
  117.5 11.6 %collective-permute-start.4 = (bf16[4,512,128]{2,1,0:T(8,128)(2,1)S(1)}, bf16[4,512,128]{2,1,0:T(8,128)(2,1)}, u32[]{:S(2)}, u32[]{:S(2)}) collective-permute-start(bf16[4,512,128]{2,1,0:T(8,128)(2,1)S(1)} %reshape.362), channel_id=1, source_target_pairs={{4,0},{8,4},{12,8},{16,12},{20,16},{24,20},{28,24},{32,28},{36,32}... | collective-permute-start | bytes 1572872 | tf_op jit(solution)/shard_map/ppermute | solution.py:17
  252.8 6.0 %copy-start.5 = (s32[2,128]{1,0:T(2,128)S(1)}, s32[2,128]{1,0:T(2,128)}, u32[]{:S(2)}) copy-start(s32[2,128]{1,0:T(2,128)} %param.22) | copy-start | bytes 3076
  252.8 6.0 %copy-start.7 = (s32[1,2]{1,0:T(1,128)S(1)}, s32[1,2]{1,0:T(1,128)}, u32[]{:S(2)}) copy-start(s32[1,2]{1,0:T(1,128)} %param.23) | copy-start | bytes 28
  252.8 118.6 %all-to-all-start.7 = ((bf16[16,2,65536]{2,1,0:T(2,128)(2,1)}), bf16[16,2,65536]{2,1,0:T(2,128)(2,1)}, u32[]{:S(2)}, u32[]{:S(2)}) async-start(bf16[16,2,65536]{2,1,0:T(2,128)(2,1)} %reshape.394), calls=%async_computation.7 | async-start | bytes 8388608 | tf_op jit(solution)/shard_map/all_to_all | solution.py:196
  257.5 139.2 %all-gather.3.cloned.1.call-start = ((), (), s32[]{:S(2)}) async-start(), calls=%async_computation.9 | async-start | bytes 4456448 | tf_op jit(solution)/shard_map/all_gather | solution.py:201
Sparse Core Ops, SparseCore 0:
  10.3 56.3 all-gather.4
Sparse Core Ops, SparseCore 1:
  260.1 110.8 all-gather.2
where the time goes:
time: 433 us; the launch traced here: 430 us
  waiting for transfers between devices  165 us (38%)
  local copies, waits for them, and re-layouts  69.7 us (16%)
  starting transfers between devices  52.6 us (12%)
  matrix products  49.4 us (11%)
  other arithmetic  40.5 us (9%)
  blocking collectives  36.2 us (8%)
  between operations  15.5 us (4%)
    all_to_all x1, waiting for transfers between devices, per_device(): lax.all_to_all(full_input, 'context', split_axis=2, concat_axis=1, tiled=...  113 us
    unnamed x27, local copies, waits for them, and re-layouts  33.5 us
    unnamed x4, other arithmetic  29.1 us
    dot_general x12, matrix products, block_grads(): jnp.einsum('ghqk,ghqd->gkd', dscores, query_blk, preferred_element_type=j...  19.9 us
    all_to_all x1, blocking collectives, per_device(): lax.all_to_all(quantized[None], 'dp', split_axis=2, concat_axis=0, tiled=...  19.2 us
    all_gather x1, local copies, waits for them, and re-layouts, per_device(): full_input = lax.all_gather(layer_input, 'tensor', axis=2, tiled=True)  18.9 us
    all_to_all x1, blocking collectives, per_device(): lax.all_to_all(outgoing, 'context', split_axis=0, concat_axis=0, tiled=True)  17 us
    all_to_all x1, waiting for transfers between devices, per_device(): lax.all_to_all(pack(key_states), 'context', split_axis=0, concat_axis=0,...  16.5 us
  transfers between devices with their start and end apart: 17, of which 6 were waited for; matrix products, arithmetic and copies ran while one was open for 22% of the time, Pallas kernels for 0%

commit v1 on v0

--- a/solution.py
+++ b/solution.py
@@ -192,7 +192,9 @@
         "rt,rx->tx", send_table, returned, preferred_element_type=jnp.float32
     ).astype(jnp.bfloat16)
     kv_local = stored_rows.reshape(local_tokens, local_cols)[None]
-    full_input = lax.all_gather(layer_input, "tensor", axis=2, tiled=True)
+    full_input = jnp.concatenate(
+        lax.all_to_all(jnp.stack([layer_input] * lax.axis_size("tensor")), "tensor", 0, 0), axis=2
+    )
     row_input = lax.all_to_all(full_input, "context", split_axis=2, concat_axis=1, tiled=True)
     span = row_input[0]
     member_grad = jnp.einsum(

time: 433 us -> 480 us (1.11)
  waiting for transfers between devices: 165 us -> 220 us
  blocking collectives: 36.2 us -> 17.6 us
  starting transfers between devices: 52.6 us -> 67.9 us
    all_to_all x0 -> x2, waiting for transfers between devices: none -> 58.6 us  [the longest x1 47.9 us: per_device(): lax.all_to_all(jnp.stack([layer_input] * lax.axis_size('tensor')), 'tenso...]
    all_gather x1 -> x0, local copies, waits for them, and re-layouts: 18.9 us -> none  [per_device(): full_input = lax.all_gather(layer_input, 'tensor', axis=2, tiled=True)]
    all_to_all x1 -> x0, blocking collectives: 17 us -> none  [per_device(): lax.all_to_all(outgoing, 'context', split_axis=0, concat_axis=0, tiled=True)]
    all_to_all x0 -> x2, starting transfers between devices: none -> 13 us  [the longest x1 6.94 us: per_device(): lax.all_to_all(jnp.stack([layer_input] * lax.axis_size('tensor')), 'tenso...]
    reshape x0 -> x1, local copies, waits for them, and re-layouts: none -> 8.63 us  [per_device(): jnp.concatenate(lax.all_to_all(jnp.stack([layer_input] * lax.axis_size('t...]
    unnamed x27 -> x25, local copies, waits for them, and re-layouts: 33.5 us -> 34.2 us
  transfers between devices with their start and end apart: 17 -> 18, of which waited for: 6 -> 8; matrix products, arithmetic and copies ran while one was open for 22% -> 10% of each run, Pallas kernels for 0% -> 0%
where the time goes in v1:
time: 480 us; the launch traced here: 476 us
  waiting for transfers between devices  220 us (46%)
  starting transfers between devices  67.9 us (14%)
  local copies, waits for them, and re-layouts  64.9 us (14%)
  matrix products  49.4 us (10%)
  other arithmetic  41.2 us (9%)
  blocking collectives  17.6 us (4%)
  between operations  14 us (3%)
    all_to_all x1, waiting for transfers between devices, per_device(): lax.all_to_all(full_input, 'context', split_axis=2, concat_axis=1, tiled=...  113 us
    all_to_all x1, waiting for transfers between devices, per_device(): lax.all_to_all(jnp.stack([layer_input] * lax.axis_size('tensor')), 'tenso...  47.9 us
    unnamed x25, local copies, waits for them, and re-layouts  34.2 us
    unnamed x4, other arithmetic  29.1 us
    dot_general x12, matrix products, block_grads(): jnp.einsum('ghqk,ghqd->gkd', dscores, query_blk, preferred_element_type=j...  19.9 us
    all_to_all x1, blocking collectives, per_device(): lax.all_to_all(quantized[None], 'dp', split_axis=2, concat_axis=0, tiled=...  17.6 us
    all_to_all x1, waiting for transfers between devices, per_device(): lax.all_to_all(pack(key_states), 'context', split_axis=0, concat_axis=0,...  16.6 us
    dot_general x12, matrix products, block_grads(): jnp.einsum('ghqd,gkd->ghqk', query_blk, key_blk, preferred_element_type=j...  15.7 us
  transfers between devices with their start and end apart: 18, of which 8 were waited for; matrix products, arithmetic and copies ran while one was open for 10% of the time, Pallas kernels for 0%

profile of v1, /device:TPU:6, one launch (start us, length us, event | category | flops | bytes accessed | tf_op | source)
XLA Modules:
  0.0 476.3 jit_solution(6131176147378753890)
XLA Ops:
  10.5 7.2 %all-to-all-start.2 = ((bf16[16,4,32]{2,1,0:T(4,128)(2,1)}), bf16[16,4,32]{2,1,0:T(4,128)(2,1)S(1)}, u32[]{:S(2)}, u32[]{:S(2)}) async-start(bf16[16,4,32]{2,1,0:T(4,128)(2,1)} %copy.68), calls=%async_computation.2 | async-start | bytes 32768 | tf_op jit(solution)/shard_map/all_to_all | solution.py:122
  25.3 5.8 %all-to-all-start.5 = ((bf16[16,4,32]{2,1,0:T(4,128)(2,1)}), bf16[16,4,32]{2,1,0:T(4,128)(2,1)S(1)}, u32[]{:S(2)}, u32[]{:S(2)}) async-start(bf16[16,4,32]{2,1,0:T(4,128)(2,1)} %copy.73), calls=%async_computation.5 | async-start | bytes 32768 | tf_op jit(solution)/shard_map/all_to_all | solution.py:123
  38.9 7.2 %all-to-all-start = ((bf16[16,4,4096]{2,1,0:T(4,128)(2,1)}), bf16[16,4,4096]{2,1,0:T(4,128)(2,1)S(1)}, u32[]{:S(2)}, u32[]{:S(2)}) async-start(bf16[16,4,4096]{2,1,0:T(4,128)(2,1)} %copy.65), calls=%async_computation | async-start | bytes 1048576 | tf_op jit(solution)/shard_map/all_to_all | solution.py:118
  46.6 15.6 %all-to-all-done = bf16[16,4,4096]{2,1,0:T(4,128)(2,1)S(1)} async-done(((bf16[16,4,4096]{2,1,0:T(4,128)(2,1)}), bf16[16,4,4096]{2,1,0:T(4,128)(2,1)S(1)}, u32[]{:S(2)}, u32[]{:S(2)}) %all-to-all-start) | async-done | bytes 524320 | tf_op jit(solution)/shard_map/all_to_all | solution.py:118
  62.2 4.2 all-to-all-start.3
  72.1 8.8 %collective-permute-done.3 = bf16[4,512]{1,0:T(4,128)(2,1)S(1)} collective-permute-done((bf16[4,512]{1,0:T(4,128)(2,1)S(1)}, bf16[4,512]{1,0:T(4,128)(2,1)S(1)}, u32[]{:S(2)}, u32[]{:S(2)}) %collective-permute-start.3) | collective-permute-done | bytes 4128 | tf_op jit(solution)/shard_map/ppermute | solution.py:17
  84.2 9.8 %all-to-all-start.1 = ((bf16[16,2,2048]{2,1,0:T(2,128)(2,1)}), bf16[16,2,2048]{2,1,0:T(2,128)(2,1)S(1)}, u32[]{:S(2)}, u32[]{:S(2)}) async-start(bf16[16,2,2048]{2,1,0:T(2,128)(2,1)} %reshape.407), calls=%async_computation.1 | async-start | bytes 262144 | tf_op jit(solution)/shard_map/all_to_all | solution.py:120
  96.1 16.6 %all-to-all-done.1 = bf16[16,2,2048]{2,1,0:T(2,128)(2,1)S(1)} async-done(((bf16[16,2,2048]{2,1,0:T(2,128)(2,1)}), bf16[16,2,2048]{2,1,0:T(2,128)(2,1)S(1)}, u32[]{:S(2)}, u32[]{:S(2)}) %all-to-all-start.1) | async-done | bytes 131104 | tf_op jit(solution)/shard_map/all_to_all | solution.py:120
  112.6 5.7 %all-to-all-start.4 = ((bf16[16,2,2048]{2,1,0:T(2,128)(2,1)}), bf16[16,2,2048]{2,1,0:T(2,128)(2,1)S(1)}, u32[]{:S(2)}, u32[]{:S(2)}) async-start(bf16[16,2,2048]{2,1,0:T(2,128)(2,1)} %reshape.409), calls=%async_computation.4 | async-start | bytes 262144 | tf_op jit(solution)/shard_map/all_to_all | solution.py:121
  120.1 6.9 %all-to-all-done.4 = bf16[16,2,2048]{2,1,0:T(2,128)(2,1)S(1)} async-done(((bf16[16,2,2048]{2,1,0:T(2,128)(2,1)}), bf16[16,2,2048]{2,1,0:T(2,128)(2,1)S(1)}, u32[]{:S(2)}, u32[]{:S(2)}) %all-to-all-start.4) | async-done | bytes 131104 | tf_op jit(solution)/shard_map/all_to_all | solution.py:121
  127.5 2.3 pad_maximum_fusion
  131.2 44.5 %while.16 = (s32[]{:T(128)}, f32[1,512,128]{2,1,0:T(8,128)S(1)}, f32[1,512,128]{2,1,0:T(8,128)S(1)}, s32[1536]{0:T(1024)S(1)}, s32[512]{0:T(512)S(1)}, /*index=5...) while((s32[]{:T(128)}, f32[1,512,128]{2,1,0:T(8,128)S(1)}, ...), condition=%wide.region_7.8_spmd.clone, body=%wide.region_6.7_spmd.clone.sunk | while | flops 270796288 | bytes 5133045 | solution.py:180
  136.5 1.7 fusion.161
  140.2 1.7 fusion.161
  151.4 1.7 fusion.161
  162.5 1.7 fusion.161
  166.2 1.7 fusion.161
  178.3 6.0 %all-to-all-start.6 = ((bf16[16,2,4096]{2,1,0:T(2,128)(2,1)}), bf16[16,2,4096]{2,1,0:T(2,128)(2,1)S(1)}, u32[]{:S(2)}, u32[]{:S(2)}) async-start(bf16[16,2,4096]{2,1,0:T(2,128)(2,1)} %reshape.411), calls=%async_computation.6 | async-start | bytes 524288 | tf_op jit(solution)/shard_map/all_to_all | solution.py:190
  184.9 10.6 %all-to-all-done.6 = bf16[16,2,4096]{2,1,0:T(2,128)(2,1)S(1)} async-done(((bf16[16,2,4096]{2,1,0:T(2,128)(2,1)}), bf16[16,2,4096]{2,1,0:T(2,128)(2,1)S(1)}, u32[]{:S(2)}, u32[]{:S(2)}) %all-to-all-start.6) | async-done | bytes 262176 | tf_op jit(solution)/shard_map/all_to_all | solution.py:190
  195.5 2.3 stack.22
  197.8 6.9 %all-to-all-start.7 = ((bf16[4,1,512,1024]{2,3,1,0:T(8,128)(2,1)}), bf16[4,1,512,1024]{2,3,1,0:T(8,128)(2,1)}, u32[]{:S(2)}, u32[]{:S(2)}) async-start(bf16[4,1,512,1024]{2,3,1,0:T(8,128)(2,1)} %stack.22), calls=%async_computation.7 | async-start | bytes 8388608 | tf_op jit(solution)/shard_map/all_to_all | solution.py:196
  205.0 47.9 %all-to-all-done.7 = bf16[4,1,512,1024]{2,3,1,0:T(8,128)(2,1)} async-done(((bf16[4,1,512,1024]{2,3,1,0:T(8,128)(2,1)}), bf16[4,1,512,1024]{2,3,1,0:T(8,128)(2,1)}, u32[]{:S(2)}, u32[]{:S(2)}) %all-to-all-start.7) | async-done | bytes 4194336 | tf_op jit(solution)/shard_map/all_to_all | solution.py:196
  252.9 8.6 %copy.111 = bf16[1,512,4096]{1,0,2:T(2,128)(2,1)} copy(bf16[1,512,4096]{1,2,0:T(8,128)(2,1)} %bitcast.29) | data formatting | bytes 8388608 | tf_op jit(solution)/shard_map/reshape | solution.py:195
  261.5 28.5 %reduce.7 = bf16[4096,512]{1,0:T(8,128)(2,1)} reduce(bf16[4096,1,512]{2,1,0:T(2,128)(2,1)} %bitcast.165, bf16[]{:T(256)} %broadcast.477), dimensions={1}, to_apply=%bitcast.154.reduce_sub_computation | reduce | bytes 8388610
  290.0 11.4 %reshape.405 = bf16[16,2,65536]{2,1,0:T(2,128)(2,1)} reshape(bf16[4096,512]{1,0:T(8,128)(2,1)} %reduce.7) | data formatting | bytes 8388608
  301.4 4.7 all-to-all-start.8
  307.5 112.5 %all-to-all-done.8 = bf16[16,2,65536]{2,1,0:T(2,128)(2,1)} async-done(((bf16[16,2,65536]{2,1,0:T(2,128)(2,1)}), bf16[16,2,65536]{2,1,0:T(2,128)(2,1)}, u32[]{:S(2)}, u32[]{:S(2)}) %all-to-all-start.8) | async-done | bytes 4194336 | tf_op jit(solution)/shard_map/all_to_all | solution.py:198
  420.0 12.3 %reshape.406 = bf16[4096,1,512]{2,1,0:T(2,128)(2,1)} reshape(bf16[16,2,65536]{2,1,0:T(2,128)(2,1)} %all-to-all-done.8) | data formatting | bytes 8388608
  432.3 6.5 %copy.89 = bf16[1,512,4096]{1,2,0:T(8,128)(2,1)} copy(bf16[1,512,4096]{1,0,2:T(2,128)(2,1)} %bitcast.166) | data formatting | bytes 8388608
  438.9 6.4 %copy.80 = bf16[1,16,512,256]{3,2,1,0:T(8,128)(2,1)} copy(bf16[1,16,512,256]{2,3,1,0:T(8,128)(2,1)} %bitcast.167) | data formatting | bytes 8388608 | tf_op jit(solution)/shard_map/all_to_all | solution.py:198
  445.3 5.2 %fusion.34 = f32[256,256]{0,1:T(8,128)S(1)} fusion(bf16[8192,256]{1,0:T(8,128)(2,1)} %bitcast.168, bf16[1,8192,256]{2,1,0:T(8,128)(2,1)} %all-gather.2.cloned.1.call-done), kind=kOutput, calls=%fused_computation.48 | convolution fusion | flops 1073741824 | bytes 8650752 | tf_op jit(solution)/shard_map/td,tc->dc/dot_general | solution.py:200
  451.2 17.6 %all_to_all.71 = bf16[1,2,128,256]{3,1,0,2:T(2,128)(2,1)S(1)} all-to-all(bf16[1,2,128,256]{3,1,0,2:T(2,128)(2,1)S(1)} %copy.82), channel_id=1, replica_groups=mesh['dp'=8,'context'=16,'tensor'=4] {'dp'}, dimensions={2} | all-to-all | bytes 262144 | tf_op jit(solution)/shard_map/all_to_all | solution.py:215
  (206 shorter events, 75.5 us)
Async XLA Ops:
  6.5 16.3 %copy-start.1 = (bf16[1,1,512,128]{3,2,1,0:T(8,128)(2,1)S(1)}, bf16[1,1,512,128]{3,2,1,0:T(8,128)(2,1)}, u32[]{:S(2)}) copy-start(bf16[1,1,512,128]{3,2,1,0:T(8,128)(2,1)} %param.16) | copy-start | bytes 393220
  6.5 16.4 %copy-start.3 = (bf16[1,4,512]{2,1,0:T(4,128)(2,1)S(1)}, bf16[1,4,512]{2,1,0:T(4,128)(2,1)}, u32[]{:S(2)}) copy-start(bf16[1,4,512]{2,1,0:T(4,128)(2,1)} %param.19) | copy-start | bytes 12292
  6.5 24.6 %copy-start.5 = (s32[1,10]{1,0:T(1,128)S(1)}, s32[1,10]{1,0:T(1,128)}, u32[]{:S(2)}) copy-start(s32[1,10]{1,0:T(1,128)} %param.20) | copy-start | bytes 124
  10.5 14.8 %all-to-all-start.2 = ((bf16[16,4,32]{2,1,0:T(4,128)(2,1)}), bf16[16,4,32]{2,1,0:T(4,128)(2,1)S(1)}, u32[]{:S(2)}, u32[]{:S(2)}) async-start(bf16[16,4,32]{2,1,0:T(4,128)(2,1)} %copy.68), calls=%async_computation.2 | async-start | bytes 32768 | tf_op jit(solution)/shard_map/all_to_all | solution.py:122
  17.7 15.4 %copy-start.2 = (s32[1,256]{1,0:T(1,128)S(1)}, s32[1,256]{1,0:T(1,128)}, u32[]{:S(2)}) copy-start(s32[1,256]{1,0:T(1,128)} %param.21) | copy-start | bytes 3076
  25.3 13.6 %all-to-all-start.5 = ((bf16[16,4,32]{2,1,0:T(4,128)(2,1)}), bf16[16,4,32]{2,1,0:T(4,128)(2,1)S(1)}, u32[]{:S(2)}, u32[]{:S(2)}) async-start(bf16[16,4,32]{2,1,0:T(4,128)(2,1)} %copy.73), calls=%async_computation.5 | async-start | bytes 32768 | tf_op jit(solution)/shard_map/all_to_all | solution.py:123
  38.9 23.3 %all-to-all-start = ((bf16[16,4,4096]{2,1,0:T(4,128)(2,1)}), bf16[16,4,4096]{2,1,0:T(4,128)(2,1)S(1)}, u32[]{:S(2)}, u32[]{:S(2)}) async-start(bf16[16,4,4096]{2,1,0:T(4,128)(2,1)} %copy.65), calls=%async_computation | async-start | bytes 1048576 | tf_op jit(solution)/shard_map/all_to_all | solution.py:118
  62.2 22.0 %all-to-all-start.3 = ((bf16[16,4,4096]{2,1,0:T(4,128)(2,1)}), bf16[16,4,4096]{2,1,0:T(4,128)(2,1)S(1)}, u32[]{:S(2)}, u32[]{:S(2)}) async-start(bf16[16,4,4096]{2,1,0:T(4,128)(2,1)} %copy.70), calls=%async_computation.3 | async-start | bytes 1048576 | tf_op jit(solution)/shard_map/all_to_all | solution.py:119
  66.7 14.2 %collective-permute-start.3 = (bf16[4,512]{1,0:T(4,128)(2,1)S(1)}, bf16[4,512]{1,0:T(4,128)(2,1)S(1)}, u32[]{:S(2)}, u32[]{:S(2)}) collective-permute-start(bf16[4,512]{1,0:T(4,128)(2,1)S(1)} %squeeze_reshape.6), channel_id=1, source_target_pairs={{8,0},{12,4},{16,8},{20,12},{24,16},{28,20},{32,24},{36,28},{40,32... | collective-permute-start | bytes 12296 | tf_op jit(solution)/shard_map/ppermute | solution.py:17
  68.0 13.0 %collective-permute-start.2 = (bf16[4,512]{1,0:T(4,128)(2,1)S(1)}, bf16[4,512]{1,0:T(4,128)(2,1)S(1)}, u32[]{:S(2)}, u32[]{:S(2)}) collective-permute-start(bf16[4,512]{1,0:T(4,128)(2,1)S(1)} %squeeze_reshape.6), channel_id=1, source_target_pairs={{4,0},{8,4},{12,8},{16,12},{20,16},{24,20},{28,24},{32,28},{36,32}... | collective-permute-start | bytes 12296 | tf_op jit(solution)/shard_map/ppermute | solution.py:17
  69.6 48.7 %collective-permute-start.7 = (bf16[4,512]{1,0:T(4,128)(2,1)S(1)}, bf16[4,512]{1,0:T(4,128)(2,1)S(1)}, u32[]{:S(2)}, u32[]{:S(2)}) collective-permute-start(bf16[4,512]{1,0:T(4,128)(2,1)S(1)} %squeeze_reshape.7), channel_id=1, source_target_pairs={{8,0},{12,4},{16,8},{20,12},{24,16},{28,20},{32,24},{36,28},{40,32... | collective-permute-start | bytes 12296 | tf_op jit(solution)/shard_map/ppermute | solution.py:17
  70.8 48.8 %collective-permute-start.6 = (bf16[4,512]{1,0:T(4,128)(2,1)S(1)}, bf16[4,512]{1,0:T(4,128)(2,1)S(1)}, u32[]{:S(2)}, u32[]{:S(2)}) collective-permute-start(bf16[4,512]{1,0:T(4,128)(2,1)S(1)} %squeeze_reshape.7), channel_id=1, source_target_pairs={{4,0},{8,4},{12,8},{16,12},{20,16},{24,20},{28,24},{32,28},{36,32}... | collective-permute-start | bytes 12296 | tf_op jit(solution)/shard_map/ppermute | solution.py:17
  81.6 45.9 %collective-permute-start.1 = (bf16[4,512,128]{2,1,0:T(8,128)(2,1)S(1)}, bf16[4,512,128]{2,1,0:T(8,128)(2,1)S(1)}, u32[]{:S(2)}, u32[]{:S(2)}) collective-permute-start(bf16[4,512,128]{2,1,0:T(8,128)(2,1)S(1)} %reshape.367), channel_id=1, source_target_pairs={{8,0},{12,4},{16,8},{20,12},{24,16},{28,20},{32,24},{36,28},{40,32... | collective-permute-start | bytes 1572872 | tf_op jit(solution)/shard_map/ppermute | solution.py:17
  82.9 44.6 %collective-permute-start = (bf16[4,512,128]{2,1,0:T(8,128)(2,1)S(1)}, bf16[4,512,128]{2,1,0:T(8,128)(2,1)}, u32[]{:S(2)}, u32[]{:S(2)}) collective-permute-start(bf16[4,512,128]{2,1,0:T(8,128)(2,1)S(1)} %reshape.367), channel_id=1, source_target_pairs={{4,0},{8,4},{12,8},{16,12},{20,16},{24,20},{28,24},{32,28},{36,32}... | collective-permute-start | bytes 1572872 | tf_op jit(solution)/shard_map/ppermute | solution.py:17
  84.2 28.4 %all-to-all-start.1 = ((bf16[16,2,2048]{2,1,0:T(2,128)(2,1)}), bf16[16,2,2048]{2,1,0:T(2,128)(2,1)S(1)}, u32[]{:S(2)}, u32[]{:S(2)}) async-start(bf16[16,2,2048]{2,1,0:T(2,128)(2,1)} %reshape.407), calls=%async_computation.1 | async-start | bytes 262144 | tf_op jit(solution)/shard_map/all_to_all | solution.py:120
  94.8 35.1 %collective-permute-start.5 = (bf16[4,512,128]{2,1,0:T(8,128)(2,1)S(1)}, bf16[4,512,128]{2,1,0:T(8,128)(2,1)}, u32[]{:S(2)}, u32[]{:S(2)}) collective-permute-start(bf16[4,512,128]{2,1,0:T(8,128)(2,1)S(1)} %reshape.371), channel_id=1, source_target_pairs={{8,0},{12,4},{16,8},{20,12},{24,16},{28,20},{32,24},{36,28},{40,32... | collective-permute-start | bytes 1572872 | tf_op jit(solution)/shard_map/ppermute | solution.py:17
  112.6 14.4 %all-to-all-start.4 = ((bf16[16,2,2048]{2,1,0:T(2,128)(2,1)}), bf16[16,2,2048]{2,1,0:T(2,128)(2,1)S(1)}, u32[]{:S(2)}, u32[]{:S(2)}) async-start(bf16[16,2,2048]{2,1,0:T(2,128)(2,1)} %reshape.409), calls=%async_computation.4 | async-start | bytes 262144 | tf_op jit(solution)/shard_map/all_to_all | solution.py:121
  118.3 11.6 %collective-permute-start.4 = (bf16[4,512,128]{2,1,0:T(8,128)(2,1)S(1)}, bf16[4,512,128]{2,1,0:T(8,128)(2,1)}, u32[]{:S(2)}, u32[]{:S(2)}) collective-permute-start(bf16[4,512,128]{2,1,0:T(8,128)(2,1)S(1)} %reshape.371), channel_id=1, source_target_pairs={{4,0},{8,4},{12,8},{16,12},{20,16},{24,20},{28,24},{32,28},{36,32}... | collective-permute-start | bytes 1572872 | tf_op jit(solution)/shard_map/ppermute | solution.py:17
  175.7 8.6 %copy-start = (bf16[1,512,1024]{2,1,0:T(8,128)(2,1)S(1)}, bf16[1,512,1024]{2,1,0:T(8,128)(2,1)}, u32[]{:S(2)}) copy-start(bf16[1,512,1024]{2,1,0:T(8,128)(2,1)} %param.13) | copy-start | bytes 3145732
  178.3 17.2 %all-to-all-start.6 = ((bf16[16,2,4096]{2,1,0:T(2,128)(2,1)}), bf16[16,2,4096]{2,1,0:T(2,128)(2,1)S(1)}, u32[]{:S(2)}, u32[]{:S(2)}) async-start(bf16[16,2,4096]{2,1,0:T(2,128)(2,1)} %reshape.411), calls=%async_computation.6 | async-start | bytes 524288 | tf_op jit(solution)/shard_map/all_to_all | solution.py:190
  197.8 55.2 %all-to-all-start.7 = ((bf16[4,1,512,1024]{2,3,1,0:T(8,128)(2,1)}), bf16[4,1,512,1024]{2,3,1,0:T(8,128)(2,1)}, u32[]{:S(2)}, u32[]{:S(2)}) async-start(bf16[4,1,512,1024]{2,3,1,0:T(8,128)(2,1)} %stack.22), calls=%async_computation.7 | async-start | bytes 8388608 | tf_op jit(solution)/shard_map/all_to_all | solution.py:196
  301.4 6.0 %copy-start.4 = (s32[2,128]{1,0:T(2,128)S(1)}, s32[2,128]{1,0:T(2,128)}, u32[]{:S(2)}) copy-start(s32[2,128]{1,0:T(2,128)} %param.22) | copy-start | bytes 3076
  301.4 6.0 %copy-start.6 = (s32[1,2]{1,0:T(1,128)S(1)}, s32[1,2]{1,0:T(1,128)}, u32[]{:S(2)}) copy-start(s32[1,2]{1,0:T(1,128)} %param.23) | copy-start | bytes 28
  301.4 118.6 %all-to-all-start.8 = ((bf16[16,2,65536]{2,1,0:T(2,128)(2,1)}), bf16[16,2,65536]{2,1,0:T(2,128)(2,1)}, u32[]{:S(2)}, u32[]{:S(2)}) async-start(bf16[16,2,65536]{2,1,0:T(2,128)(2,1)} %reshape.405), calls=%async_computation.8 | async-start | bytes 8388608 | tf_op jit(solution)/shard_map/all_to_all | solution.py:198
  306.1 139.2 %all-gather.2.cloned.1.call-start = ((), (), s32[]{:S(2)}) async-start(), calls=%async_computation.10 | async-start | bytes 4456448 | tf_op jit(solution)/shard_map/all_gather | solution.py:203
Sparse Core Ops, SparseCore 0:
  309.1 108.4 all-gather.1
